TPU v7x, 256 devices: a whole 4x4x8 slice. The times are simulated.
256 devices in a mesh: tm: 8 (over z), seq: 32 (over y, x, core).
Axes of the slice: x: 4, y: 4, z: 8, core: 2. Of those that a mesh axis runs over, the one named last changes fastest.
Arguments:
- states: float32 [64, 1536, 64], P('tm', 'seq'), may hold values from -11 to 11
- first_state: float32 [1536, 64], P('seq'), may hold values from -6 to 6
- now_step: int32 [64], P('tm'), may hold values from 1 to 960, as said below
- next_step: int32 [64], P('tm'), may hold values from 0 to 959, as said below
- embed_weight: bfloat16 [64, 1536], replicated, may hold values from -0.75 to 0.75
- mod_weight: bfloat16 [256, 4608], replicated, may hold values from -0.375 to 0.375
- qkv_weight: bfloat16 [1536, 12, 384], P('seq'), may hold values from -1 to 1
- out_weight: bfloat16 [1536, 1536], P('seq'), may hold values from -0.15625 to 0.15625
- final_weight: bfloat16 [1536, 64], replicated, may hold values from -0.15625 to 0.15625
Outputs:
- advanced: float32 [64, 1536, 64], P('tm', 'seq')
- errors: float32 [64], P('tm')
Inputs may be any that keep to these rules, and one draw needn't show every extreme that they name: now_step[0] = 960 and now_step[j + 1] = next_step[j]. next_step[j] is now_step[j] minus a gap of 1 to 15.
All inputs are finite; a program needn't handle non-finite values.
Results may differ from a plain program's by a relative error of at most 0.002.
Values may be sent and summed in bfloat16 or wider, within the bound.
A program may use at most 64 MiB of HBM per device.

v0:
```python
import math
import jax
import jax.numpy as jnp
from jax import lax
from jax.sharding import PartitionSpec as P


def from_behind(shard, axis, by):
    count = lax.axis_size(axis)
    pairs = [(i, i + by) for i in range(count) if 0 <= i + by < count]
    return lax.ppermute(shard, axis, pairs)


def entering(part, axis, combine, identity):
    place = lax.axis_index(axis)
    gathered = lax.all_gather(part, axis)
    state = jnp.zeros_like(part) + jnp.asarray(identity, part.dtype)

    def one(step, state):
        return combine(state, lax.dynamic_index_in_dim(gathered, step, 0, False))

    return lax.fori_loop(0, place, one, state)


def layer_norm(rows):
    row_mean = jnp.mean(rows, axis=-1, keepdims=True)
    centered = rows - row_mean
    variance = jnp.mean(centered * centered, axis=-1, keepdims=True)
    return centered * lax.rsqrt(variance + 1e-06)


def alpha_bar(step_ids):
    fraction = (step_ids.astype(jnp.float32) / 1000.0 + 0.008) / 1.008
    return jnp.cos(fraction * (math.pi / 2)) ** 2


def coefficients(now_step, next_step):
    alpha_now = alpha_bar(now_step)
    alpha_next = alpha_bar(next_step)
    step_ratio = jnp.sqrt(alpha_next / alpha_now)
    keep_coef = step_ratio - 1.0
    noise_coef = jnp.sqrt(1.0 - alpha_next) - step_ratio * jnp.sqrt(1.0 - alpha_now)
    return (keep_coef, noise_coef)


def modulation(step_ids, mod_weight):
    half_freq = mod_weight.shape[0] // 2
    frequency = jnp.exp(-math.log(10000.0) * jnp.arange(half_freq, dtype=jnp.float32) / half_freq)
    angles = step_ids.astype(jnp.float32)[:, None] * frequency[None, :]
    time_embed = jnp.concatenate([jnp.cos(angles), jnp.sin(angles)], axis=1).astype(jnp.bfloat16)
    return jnp.dot(time_embed, mod_weight, preferred_element_type=jnp.float32)


def attend_one(pair_item):
    hdim = pair_item.shape[1] // 3
    length = pair_item.shape[0]
    query_rows = 512
    queries = pair_item[:, :hdim]
    key_rows = pair_item[:, hdim : 2 * hdim]
    values = pair_item[:, 2 * hdim :]

    def one_block(query_block):
        scores = jnp.dot(query_block, key_rows.T, preferred_element_type=jnp.float32) * hdim ** (
            -0.5
        )
        row_max = jnp.max(scores, axis=1, keepdims=True)
        exponent = jnp.exp(scores - row_max)
        weights = (exponent / jnp.sum(exponent, axis=1, keepdims=True)).astype(jnp.bfloat16)
        return jnp.dot(weights, values, preferred_element_type=jnp.float32).astype(jnp.bfloat16)

    blocks_out = lax.map(one_block, queries.reshape(length // query_rows, query_rows, hdim))
    return blocks_out.reshape(length, hdim)


def attend_pairs(pair_block):
    return lax.map(attend_one, pair_block[0])[None]


def add_terms(earlier, later):
    return earlier + later


def per_device(
    states,
    first_state,
    now_step,
    next_step,
    embed_weight,
    mod_weight,
    qkv_weight,
    out_weight,
    final_weight,
):
    step_count, tokd, chans = states.shape
    seq_devs = lax.axis_size("seq")
    time_index = lax.axis_index("tm")
    heads = qkv_weight.shape[1]
    width_three = qkv_weight.shape[2]
    hdim = width_three // 3
    width = heads * hdim
    edge_state = from_behind(states[-1], "tm", 1)
    opening = jnp.where(time_index == 0, first_state, edge_state)
    previous = jnp.concatenate([opening[None], states[:-1]], axis=0)
    keep_coef, noise_coef = coefficients(now_step, next_step)
    modulated_all = modulation(now_step, mod_weight)
    shift_mod = modulated_all[:, :width]
    scale_mod = modulated_all[:, width : 2 * width]
    gate_mod = modulated_all[:, 2 * width :]
    residual = jnp.einsum(
        "tsc,cd->tsd",
        previous.astype(jnp.bfloat16),
        embed_weight,
        preferred_element_type=jnp.float32,
    )
    modulated = (
        layer_norm(residual) * (1.0 + scale_mod[:, None, :]) + shift_mod[:, None, :]
    ).astype(jnp.bfloat16)
    columns = modulated
    projected = jnp.einsum(
        "tsd,dhc->thsc",
        columns,
        lax.all_gather(qkv_weight, "seq", axis=0, tiled=True),
        preferred_element_type=jnp.float32,
    ).astype(jnp.bfloat16)
    pair_count = step_count * heads
    per_dev = pair_count // seq_devs
    grouped = projected.reshape(seq_devs, per_dev, tokd, width_three)
    routed = attend_pairs(lax.all_to_all(grouped, "seq", split_axis=0, concat_axis=2, tiled=True))
    returned = lax.all_to_all(routed, "seq", split_axis=2, concat_axis=0, tiled=True)
    flattened = jnp.transpose(
        returned.reshape(step_count, heads, tokd, hdim), (0, 2, 1, 3)
    ).reshape(step_count, tokd, width)
    columns = flattened
    projection = jnp.einsum(
        "tsd,de->tse",
        columns,
        lax.all_gather(out_weight, "seq", axis=0, tiled=True),
        preferred_element_type=jnp.float32,
    )
    updated = residual + gate_mod[:, None, :] * projection
    normed_out = layer_norm(updated).astype(jnp.bfloat16)
    noise_pred = jnp.einsum(
        "tsd,dc->tsc", normed_out, final_weight, preferred_element_type=jnp.float32
    )
    drift_terms = keep_coef[:, None, None] * previous + noise_coef[:, None, None] * noise_pred
    running_sums = jnp.cumsum(drift_terms, axis=0)
    block_total = running_sums[-1]
    carried = entering(block_total, "tm", add_terms, jnp.zeros_like(block_total))
    advanced = first_state[None] + carried[None] + running_sums
    difference = advanced - states
    partial_value = jnp.sum(difference * difference, axis=(1, 2))
    errors = lax.psum(partial_value, "seq") / (tokd * seq_devs * chans)
    return (advanced, errors)


def solution(mesh):
    in_specs = (
        P("tm", "seq", None),
        P("seq", None),
        P("tm"),
        P("tm"),
        P(),
        P(),
        P("seq", None, None),
        P("seq", None),
        P(),
    )
    out_specs = (P("tm", "seq", None), P("tm"))
    return jax.shard_map(
        per_device, mesh=mesh, in_specs=in_specs, out_specs=out_specs, check_vma=False
    )
```

profile of v0, /device:TPU:1, one launch (start us, length us, event | category | flops | bytes accessed | tf_op | source)
XLA Modules:
  0.0 330.8 jit_solution(13507943861712329472)
XLA Ops:
  7.3 0.7 all-gather.3.cloned.1.call-update
  7.9 0.8 slice_bitcast_fusion
  8.8 4.3 %collective-permute-start = (f32[48,64]{1,0:T(8,128)S(1)}, f32[48,64]{1,0:T(8,128)S(1)}, u32[]{:S(2)}, u32[]{:S(2)}) collective-permute-start(f32[48,64]{1,0:T(8,128)S(1)} %slice_bitcast_fusion), channel_id=1, source_target_pairs={{0,32},{32,64},{64,96},{96,128},{128,160},{160,192},{192,224},{1,3... | collective-permute-start | bytes 36872 | tf_op jit(solution)/shard_map/ppermute | solution.py:11
  13.1 0.7 convert_element_type.30
  14.3 0.6 fusion.53
  16.2 1.4 copy-done.1
  18.0 68.3 %all-gather.3.cloned.1.call-done = bf16[1536,12,384]{2,0,1:T(8,128)(2,1)} async-done(((bf16[48,12,384]{2,0,1:T(8,128)(2,1)}), bf16[1536,12,384]{2,0,1:T(8,128)(2,1)}) %all-gather.3.cloned.1.call-update) | async-done | bytes 14155792 | tf_op jit(solution)/shard_map/all_gather | solution.py:122
  86.3 11.1 %fusion.18 = bf16[8,48,12,384]{3,1,2,0:T(8,128)(2,1)} fusion(bf16[1536,12,384]{2,0,1:T(8,128)(2,1)} %all-gather.3.cloned.1.call-done, f32[8,48,1536]{2,1,0:T(8,128)} %copy-done.1, f32[8,1536]{1,0:T(8,128)S(1)} %get-tuple-element.105, f32[8,1536]{1,0:T(8,128)S(1)} %get-tuple-element.106, f32[8,48]{1,0:T(8,128)S(1)} %add_rsqrt_fusion.1, ...), kind=kOutput, calls=%fused_computation.20 | convolution fusion | flops 5440536576 | bytes 20155392 | tf_op jit(solution)/shard_map/tsd,dhc->thsc/dot_general | solution.py:119
  97.3 5.5 %all-to-all-start = ((bf16[32,3,48,384]{3,2,1,0:T(8,128)(2,1)}), bf16[32,3,48,384]{3,2,1,0:T(8,128)(2,1)}, u32[]{:S(2)}, u32[]{:S(2)}) async-start(bf16[32,3,48,384]{3,2,1,0:T(8,128)(2,1)} %bitcast.93), calls=%async_computation | async-start | bytes 7077888 | tf_op jit(solution)/shard_map/all_to_all | solution.py:128
  102.8 0.7 all-gather.5.cloned.1.call-update
  103.6 44.9 %all-to-all-done = bf16[32,3,48,384]{3,2,1,0:T(8,128)(2,1)} async-done(((bf16[32,3,48,384]{3,2,1,0:T(8,128)(2,1)}), bf16[32,3,48,384]{3,2,1,0:T(8,128)(2,1)}, u32[]{:S(2)}, u32[]{:S(2)}) %all-to-all-start) | async-done | bytes 3538976 | tf_op jit(solution)/shard_map/all_to_all | solution.py:128
  148.5 4.1 %copy.17 = bf16[1,3,32,48,384]{4,3,2,1,0:T(8,128)(2,1)} copy(bf16[1,3,32,48,384]{4,3,1,2,0:T(8,128)(2,1)} %bitcast.15) | data formatting | bytes 7077888 | tf_op jit(solution)/shard_map/all_to_all | solution.py:128
  152.6 33.7 %while.31 = (s32[]{:T(128)}, bf16[3,1536,128]{2,1,0:T(8,128)(2,1)}, bf16[3,1536,384]{2,1,0:T(8,128)(2,1)}, s32[]{:T(128)}, s32[]{:T(128)}, /*index=5*/s32[]{:T(128)}) while((s32[]{:T(128)}, bf16[3,1536,128]{2,1,0:T(8,128)(2,1)}, bf16[3,1536,384]{2,1,0:T(8,128)(2,1)}, s32[]{:T(128)}, s32[]{:T(128)}, /*index=5*/s32[]{:T(128)}) %tuple.79), condition=%wide.region_7.8_spmd, body=%wide.region_2.7_spmd.sunk | while | flops 408222720 | bytes 16002250 | solution.py:76
  152.6 1.4 dynamic-slice_bitcast_fusion.2
  154.2 7.8 %while.33 = (s32[]{:T(128)}, bf16[3,512,128]{2,1,0:T(8,128)(2,1)}, bf16[3,512,128]{2,1,0:T(8,128)(2,1)S(1)}, bf16[1536,128]{1,0:T(8,128)(2,1)S(1)}, bf16[1536,128]{1,0:T(8,128)(2,1)S(1)}, /*index=5*/s32[]{:T(128)}) while((s32[]{:T(128)}, bf16[3,512,128]{2,1,0:T(8,128)(2,1)}, bf16[3,512,128]{2,1,0:T(8,128)(2,1)S(1)}, ...), condition=%wide.region_6.6_spmd, body=%wide.region_3.5_spmd.sunk | while | flops 408222720 | bytes 10496585 | solution.py:71
  154.2 0.7 fusion.68
  155.5 1.4 fusion.70
  156.8 0.7 fusion.68
  158.1 1.4 fusion.70
  159.5 0.7 fusion.68
  160.7 1.4 fusion.70
  162.1 1.8 bitcast_dynamic-update-slice_fusion.2
  163.8 1.4 dynamic-slice_bitcast_fusion.2
  165.5 7.8 %while.33 = (s32[]{:T(128)}, bf16[3,512,128]{2,1,0:T(8,128)(2,1)}, bf16[3,512,128]{2,1,0:T(8,128)(2,1)S(1)}, bf16[1536,128]{1,0:T(8,128)(2,1)S(1)}, bf16[1536,128]{1,0:T(8,128)(2,1)S(1)}, /*index=5*/s32[]{:T(128)}) while((s32[]{:T(128)}, bf16[3,512,128]{2,1,0:T(8,128)(2,1)}, bf16[3,512,128]{2,1,0:T(8,128)(2,1)S(1)}, ...), condition=%wide.region_6.6_spmd, body=%wide.region_3.5_spmd.sunk | while | flops 408222720 | bytes 10496585 | solution.py:71
  165.5 0.7 fusion.68
  166.7 1.4 fusion.70
  168.1 0.7 fusion.68
  169.3 1.4 fusion.70
  170.7 0.7 fusion.68
  171.9 1.4 fusion.70
  173.3 1.8 bitcast_dynamic-update-slice_fusion.2
  175.1 1.4 dynamic-slice_bitcast_fusion.2
  176.7 7.8 %while.33 = (s32[]{:T(128)}, bf16[3,512,128]{2,1,0:T(8,128)(2,1)}, bf16[3,512,128]{2,1,0:T(8,128)(2,1)S(1)}, bf16[1536,128]{1,0:T(8,128)(2,1)S(1)}, bf16[1536,128]{1,0:T(8,128)(2,1)S(1)}, /*index=5*/s32[]{:T(128)}) while((s32[]{:T(128)}, bf16[3,512,128]{2,1,0:T(8,128)(2,1)}, bf16[3,512,128]{2,1,0:T(8,128)(2,1)S(1)}, ...), condition=%wide.region_6.6_spmd, body=%wide.region_3.5_spmd.sunk | while | flops 408222720 | bytes 10496585 | solution.py:71
  176.7 0.7 fusion.68
  177.9 1.4 fusion.70
  179.3 0.7 fusion.68
  180.6 1.4 fusion.70
  181.9 0.7 fusion.68
  183.2 1.4 fusion.70
  184.6 1.8 bitcast_dynamic-update-slice_fusion.2
  186.3 8.1 %copy.31 = bf16[3,1536,128]{2,0,1:T(4,128)(2,1)} copy(bf16[3,1536,128]{2,1,0:T(8,128)(2,1)} %get-tuple-element.69) | data formatting | bytes 2359296 | tf_op jit(solution)/shard_map/while | solution.py:76
  194.4 7.4 %all-to-all-start.1 = ((bf16[1,3,1536,128]{3,1,0,2:T(4,128)(2,1)}), bf16[1,3,1536,128]{3,1,0,2:T(4,128)(2,1)}, u32[]{:S(2)}, u32[]{:S(2)}) async-start(bf16[1,3,1536,128]{3,1,0,2:T(4,128)(2,1)} %bitcast.91), calls=%async_computation.1 | async-start | bytes 3145728 | tf_op jit(solution)/shard_map/all_to_all | solution.py:129
  202.0 22.2 %all-to-all-done.1 = bf16[1,3,1536,128]{3,1,0,2:T(4,128)(2,1)} async-done(((bf16[1,3,1536,128]{3,1,0,2:T(4,128)(2,1)}), bf16[1,3,1536,128]{3,1,0,2:T(4,128)(2,1)}, u32[]{:S(2)}, u32[]{:S(2)}) %all-to-all-start.1) | async-done | bytes 1179680 | tf_op jit(solution)/shard_map/all_to_all | solution.py:129
  224.2 1.6 copy.19
  225.9 5.1 %fusion.55 = (f32[8,48]{1,0:T(8,128)S(1)}, f32[8,48,1536]{2,1,0:T(8,128)S(1)}) fusion(f32[8,48,1536]{2,1,0:T(8,128)} %copy-done.1, bf16[1536,1536]{1,0:T(8,128)(2,1)} %all-gather.5.cloned.1.call-done, bf16[8,12,6,8,128]{4,3,2,1,0:T(8,128)(2,1)S(1)} %bitcast.94, f32[8,1536]{1,0:T(8,128)} %get-tuple-element.104), kind=kOutput, calls=%fused_computation.77 | convolution fusion | flops 1813708416 | bytes 10667520 | tf_op jit(solution)/shard_map/tsd,de->tse/dot_general | solution.py:134
  232.6 20.1 %all_gather.11 = f32[8,48,64]{2,1,0:T(8,128)S(1)} all-gather(f32[1,48,64]{2,1,0:T(8,128)S(1)} %slice.39), channel_id=1, replica_groups=mesh['tm'=8,'seq'=32] {'tm'}, dimensions={0}, use_global_device_ids=true | all-gather | bytes 110592 | tf_op jit(solution)/shard_map/all_gather | solution.py:16
  252.8 0.7 multiply_reduce_fusion.2
  253.5 70.0 %psum.7 = f32[8]{0:T(128)S(1)} all-reduce(f32[8]{0:T(128)S(1)} %get-tuple-element.95), channel_id=1, replica_groups=mesh['tm'=8,'seq'=32] {'seq'}, use_global_device_ids=true, to_apply=%region_14.15 | all-reduce | flops 8 | bytes 64 | tf_op jit(solution)/shard_map/psum | solution.py:152
  (69 shorter events, 10.2 us)
Async XLA Ops:
  7.2 6.7 %copy-start = (bf16[256,4608]{1,0:T(8,128)(2,1)S(1)}, bf16[256,4608]{1,0:T(8,128)(2,1)}, u32[]{:S(2)}) copy-start(bf16[256,4608]{1,0:T(8,128)(2,1)} %param.20) | copy-start | bytes 7077892
  7.2 7.8 %copy-start.4 = (f32[8,48,64]{2,1,0:T(8,128)S(1)}, f32[8,48,64]{2,1,0:T(8,128)}, u32[]{:S(2)}) copy-start(f32[8,48,64]{2,1,0:T(8,128)} %param.15) | copy-start | bytes 294916
  7.2 7.8 %copy-start.10 = (f32[48,64]{1,0:T(8,128)S(1)}, f32[48,64]{1,0:T(8,128)}, u32[]{:S(2)}) copy-start(f32[48,64]{1,0:T(8,128)} %param.16) | copy-start | bytes 36868
  7.2 8.4 %copy-start.9 = (bf16[64,1536]{1,0:T(8,128)(2,1)S(1)}, bf16[64,1536]{1,0:T(8,128)(2,1)}, u32[]{:S(2)}) copy-start(bf16[64,1536]{1,0:T(8,128)(2,1)} %param.19) | copy-start | bytes 589828
  7.2 79.0 %all-gather.3.cloned.1.call-start = ((), (), s32[]{:S(2)}) async-start(), calls=%async_computation.2 | async-start | bytes 14598144 | tf_op jit(solution)/shard_map/all_gather | solution.py:122
  8.8 6.2 %collective-permute-start = (f32[48,64]{1,0:T(8,128)S(1)}, f32[48,64]{1,0:T(8,128)S(1)}, u32[]{:S(2)}, u32[]{:S(2)}) collective-permute-start(f32[48,64]{1,0:T(8,128)S(1)} %slice_bitcast_fusion), channel_id=1, source_target_pairs={{0,32},{32,64},{64,96},{96,128},{128,160},{160,192},{192,224},{1,3... | collective-permute-start | bytes 36872 | tf_op jit(solution)/shard_map/ppermute | solution.py:11
  15.0 3.0 copy-start.2
  15.0 0.6 copy-start.6
  16.2 1.4 copy-start.1
  97.3 51.2 %all-to-all-start = ((bf16[32,3,48,384]{3,2,1,0:T(8,128)(2,1)}), bf16[32,3,48,384]{3,2,1,0:T(8,128)(2,1)}, u32[]{:S(2)}, u32[]{:S(2)}) async-start(bf16[32,3,48,384]{3,2,1,0:T(8,128)(2,1)} %bitcast.93), calls=%async_computation | async-start | bytes 7077888 | tf_op jit(solution)/shard_map/all_to_all | solution.py:128
  102.8 123.1 %all-gather.5.cloned.1.call-start = ((), (), s32[]{:S(2)}) async-start(), calls=%async_computation.3 | async-start | bytes 4866048 | tf_op jit(solution)/shard_map/all_gather | solution.py:137
  186.3 15.5 %copy-start.12 = (s32[8]{0:T(128)S(1)}, s32[8]{0:T(128)}, u32[]{:S(2)}) copy-start(s32[8]{0:T(128)} %param.17) | copy-start | bytes 100
  186.3 15.5 %copy-start.13 = (s32[8]{0:T(128)S(1)}, s32[8]{0:T(128)}, u32[]{:S(2)}) copy-start(s32[8]{0:T(128)} %param.18) | copy-start | bytes 100
  194.4 29.8 %all-to-all-start.1 = ((bf16[1,3,1536,128]{3,1,0,2:T(4,128)(2,1)}), bf16[1,3,1536,128]{3,1,0,2:T(4,128)(2,1)}, u32[]{:S(2)}, u32[]{:S(2)}) async-start(bf16[1,3,1536,128]{3,1,0,2:T(4,128)(2,1)} %bitcast.91), calls=%async_computation.1 | async-start | bytes 3145728 | tf_op jit(solution)/shard_map/all_to_all | solution.py:129
  231.0 0.9 copy-start.8
  231.1 1.5 copy-start.3
  231.1 1.4 copy-start.7
  231.5 21.3 %copy-start.11 = (f32[48,64]{1,0:T(8,128)S(1)}, f32[48,64]{1,0:T(8,128)}, u32[]{:S(2)}) copy-start(f32[48,64]{1,0:T(8,128)} %param.16) | copy-start | bytes 36868
  231.5 21.3 %copy-start.5 = (f32[8,48,64]{2,1,0:T(8,128)S(1)}, f32[8,48,64]{2,1,0:T(8,128)}, u32[]{:S(2)}) copy-start(f32[8,48,64]{2,1,0:T(8,128)} %param.15) | copy-start | bytes 294916
Sparse Core Ops, SparseCore 0:
  10.7 75.5 all-gather.2
  106.2 68.7 all-gather.4
where the time goes:
time: 331 us
  waiting for transfers between devices  137 us (41%)
  blocking collectives  90.1 us (27%)
  matrix products  36 us (11%)
  local copies, waits for them, and re-layouts  27.4 us (8%)
  starting transfers between devices  17.3 us (5%)
  between operations  14.4 us (4%)
  other arithmetic  8.79 us (3%)
    psum x1, blocking collectives, per_device(): errors = lax.psum(partial_value, 'seq') / (tokd * seq_devs * chans)  70 us
    all_gather x1, waiting for transfers between devices, per_device(): lax.all_gather(qkv_weight, 'seq', axis=0, tiled=True)  68.3 us
    all_to_all x1, waiting for transfers between devices, per_device(): lax.all_to_all(grouped, 'seq', split_axis=0, concat_axis=2, tiled=True)  44.9 us
    all_to_all x1, waiting for transfers between devices, per_device(): lax.all_to_all(routed, 'seq', split_axis=2, concat_axis=0, tiled=True)  22.2 us
    all_gather x1, blocking collectives, entering(): gathered = lax.all_gather(part, axis)  20.1 us
    dot_general x9, matrix products, one_block(): jnp.dot(weights, values, preferred_element_type=jnp.float32)  12.4 us
    dot_general x1, matrix products, per_device(): jnp.einsum('tsd,dhc->thsc', columns, lax.all_gather(qkv_weight, 'seq', ax...  11.1 us
    while x1, local copies, waits for them, and re-layouts, attend_pairs(): return lax.map(attend_one, pair_block[0])[None]  8.06 us
  transfers between devices with their start and end apart: 5, of which 3 were waited for; matrix products, arithmetic and copies ran while one was open for 15% of the time, Pallas kernels for 0%

commit v1 on v0

--- a/solution.py
+++ b/solution.py
@@ -3,6 +3,11 @@
 import jax.numpy as jnp
 from jax import lax
 from jax.sharding import PartitionSpec as P
+
+
+def tiled_gather(x, axis, dim):
+    copies = jnp.concatenate([x] * lax.axis_size(axis), axis=dim)
+    return lax.all_to_all(copies, axis, dim, dim, tiled=True)
 
 
 def from_behind(shard, axis, by):
@@ -119,7 +124,7 @@
     projected = jnp.einsum(
         "tsd,dhc->thsc",
         columns,
-        lax.all_gather(qkv_weight, "seq", axis=0, tiled=True),
+        tiled_gather(qkv_weight, "seq", 0),
         preferred_element_type=jnp.float32,
     ).astype(jnp.bfloat16)
     pair_count = step_count * heads

time: 331 us -> 550 us (1.66)
  waiting for transfers between devices: 137 us -> 288 us
  local copies, waits for them, and re-layouts: 27.4 us -> 73.8 us
  starting transfers between devices: 17.3 us -> 37.2 us
    all_to_all x0 -> x1, waiting for transfers between devices: none -> 221 us  [tiled_gather(): return lax.all_to_all(copies, axis, dim, dim, tiled=True)]
    all_gather x1 -> x0, waiting for transfers between devices: 68.3 us -> none  [per_device(): lax.all_gather(qkv_weight, 'seq', axis=0, tiled=True)]
    unnamed x28 -> x67, local copies, waits for them, and re-layouts: 2.57 us -> 48 us
    all_to_all x1, starting transfers between devices: 5.48 us -> 17.3 us  [per_device(): lax.all_to_all(grouped, 'seq', split_axis=0, concat_axis=2, tiled=True)]
    all_to_all x0 -> x1, starting transfers between devices: none -> 8.77 us  [tiled_gather(): return lax.all_to_all(copies, axis, dim, dim, tiled=True)]
  transfers between devices with their start and end apart: 5 -> 5, of which waited for: 3 -> 3; matrix products, arithmetic and copies ran while one was open for 15% -> 7% of each run, Pallas kernels for 0% -> 0%
where the time goes in v1:
time: 550 us; the launch traced here: 549 us
  waiting for transfers between devices  288 us (52%)
  blocking collectives  93 us (17%)
  local copies, waits for them, and re-layouts  73.8 us (13%)
  starting transfers between devices  37.2 us (7%)
  matrix products  34.4 us (6%)
  between operations  14.4 us (3%)
  other arithmetic  8.12 us (1%)
    all_to_all x1, waiting for transfers between devices, tiled_gather(): return lax.all_to_all(copies, axis, dim, dim, tiled=True)  221 us
    psum x1, blocking collectives, per_device(): errors = lax.psum(partial_value, 'seq') / (tokd * seq_devs * chans)  70.3 us
    unnamed x67, local copies, waits for them, and re-layouts  48 us
    all_to_all x1, waiting for transfers between devices, per_device(): lax.all_to_all(grouped, 'seq', split_axis=0, concat_axis=2, tiled=True)  44.5 us
    all_gather x1, blocking collectives, entering(): gathered = lax.all_gather(part, axis)  22.7 us
    all_to_all x1, waiting for transfers between devices, per_device(): lax.all_to_all(routed, 'seq', split_axis=2, concat_axis=0, tiled=True)  22.2 us
    all_to_all x1, starting transfers between devices, per_device(): lax.all_to_all(grouped, 'seq', split_axis=0, concat_axis=2, tiled=True)  17.3 us
    dot_general x1, matrix products, per_device(): jnp.einsum('tsd,dhc->thsc', columns, tiled_gather(qkv_weight, 'seq', 0),...  14.6 us
  transfers between devices with their start and end apart: 5, of which 3 were waited for; matrix products, arithmetic and copies ran while one was open for 7% of the time, Pallas kernels for 0%

profile of v1, /device:TPU:1, one launch (start us, length us, event | category | flops | bytes accessed | tf_op | source)
XLA Modules:
  0.0 549.1 jit_solution(7098229690573559362)
XLA Ops:
  7.2 2.1 copy_dynamic-update-slice_fusion.30
  9.3 1.9 copy_dynamic-update-slice_fusion.29
  11.2 1.9 copy_dynamic-update-slice_fusion.28
  13.2 1.9 copy_dynamic-update-slice_fusion.27
  15.1 1.9 copy_dynamic-update-slice_fusion.26
  17.1 1.9 copy_dynamic-update-slice_fusion.25
  19.0 1.9 copy_dynamic-update-slice_fusion.24
  20.9 1.9 copy_dynamic-update-slice_fusion.23
  22.9 1.9 copy_dynamic-update-slice_fusion.22
  24.8 1.9 copy_dynamic-update-slice_fusion.21
  26.8 2.0 copy_dynamic-update-slice_fusion.20
  28.8 2.0 copy_dynamic-update-slice_fusion.19
  30.8 1.9 copy_dynamic-update-slice_fusion.18
  32.7 1.9 copy_dynamic-update-slice_fusion.17
  34.6 2.0 copy_dynamic-update-slice_fusion.16
  36.6 1.9 copy_dynamic-update-slice_fusion.15
  38.5 1.9 copy_dynamic-update-slice_fusion.14
  40.4 1.9 copy_dynamic-update-slice_fusion.13
  42.4 1.0 copy_dynamic-update-slice_fusion.12
  47.1 1.0 copy_dynamic-update-slice_fusion.7
  48.0 0.9 copy_dynamic-update-slice_fusion.6
  49.9 1.0 copy_dynamic-update-slice_fusion.4
  50.8 0.9 copy_dynamic-update-slice_fusion.3
  51.8 0.9 copy_dynamic-update-slice_fusion.2
  54.6 0.9 copy_dynamic-update-slice_fusion.31
  55.5 8.8 %all-to-all-start = ((bf16[1536,12,384]{2,1,0:T(8,128)(2,1)}), bf16[1536,12,384]{2,1,0:T(8,128)(2,1)}, u32[]{:S(2)}, u32[]{:S(2)}) async-start(bf16[1536,12,384]{2,1,0:T(8,128)(2,1)} %copy_dynamic-update-slice_fusion.31), calls=%async_computation | async-start | bytes 37748736 | tf_op jit(solution)/shard_map/all_to_all | solution.py:10
  64.3 3.7 collective-permute-start
  70.8 220.8 %all-to-all-done = bf16[1536,12,384]{2,1,0:T(8,128)(2,1)} async-done(((bf16[1536,12,384]{2,1,0:T(8,128)(2,1)}), bf16[1536,12,384]{2,1,0:T(8,128)(2,1)}, u32[]{:S(2)}, u32[]{:S(2)}) %all-to-all-start) | async-done | bytes 14155808 | tf_op jit(solution)/shard_map/all_to_all | solution.py:10
  291.6 14.6 %convert_bitcast_fusion = bf16[8,12,48,384]{3,2,0,1:T(8,128)(2,1)} fusion(bf16[1536,12,384,1]{2,1,0,3:T(8,128)(2,1)} %bitcast.9, f32[8,48,1536]{2,1,0:T(8,128)S(1)} %get-tuple-element.110, f32[8,1536]{1,0:T(8,128)S(1)} %get-tuple-element.105, f32[8,1536]{1,0:T(8,128)S(1)} %get-tuple-element.106, f32[8,48]{1,0:T(8,128)S(1)} %add_rsqrt_fusion.1, ...), kind=kOutput, calls=%fused_computation.18 | convolution fusion | flops 5440536576 | bytes 20155392 | tf_op jit(solution)/shard_map/tsd,dhc->thsc/dot_general | solution.py:124
  306.2 4.2 copy.50
  310.3 17.3 %all-to-all-start.1 = ((bf16[32,3,48,384]{3,2,1,0:T(8,128)(2,1)}), bf16[32,3,48,384]{3,2,1,0:T(8,128)(2,1)S(1)}, u32[]{:S(2)}, u32[]{:S(2)}) async-start(bf16[32,3,48,384]{3,2,1,0:T(8,128)(2,1)} %bitcast.85), calls=%async_computation.1 | async-start | bytes 7077888 | tf_op jit(solution)/shard_map/all_to_all | solution.py:133
  328.4 44.5 %all-to-all-done.1 = bf16[32,3,48,384]{3,2,1,0:T(8,128)(2,1)S(1)} async-done(((bf16[32,3,48,384]{3,2,1,0:T(8,128)(2,1)}), bf16[32,3,48,384]{3,2,1,0:T(8,128)(2,1)S(1)}, u32[]{:S(2)}, u32[]{:S(2)}) %all-to-all-start.1) | async-done | bytes 3538976 | tf_op jit(solution)/shard_map/all_to_all | solution.py:133
  373.0 2.1 copy.51
  375.1 25.9 %while.31 = (s32[]{:T(128)}, bf16[3,1536,128]{2,1,0:T(8,128)(2,1)}, bf16[3,1536,384]{2,1,0:T(8,128)(2,1)}, s32[]{:T(128)}, s32[]{:T(128)}, /*index=5*/s32[]{:T(128)}) while((s32[]{:T(128)}, bf16[3,1536,128]{2,1,0:T(8,128)(2,1)}, bf16[3,1536,384]{2,1,0:T(8,128)(2,1)}, s32[]{:T(128)}, s32[]{:T(128)}, /*index=5*/s32[]{:T(128)}) %tuple.68), condition=%wide.region_7.8_spmd, body=%wide.region_2.7_spmd.sunk | while | flops 408222720 | bytes 16001742 | solution.py:81
  375.1 1.4 dynamic-slice_bitcast_fusion.2
  376.7 6.1 %while.33 = (s32[]{:T(128)}, bf16[3,512,128]{2,1,0:T(8,128)(2,1)S(1)}, bf16[3,512,128]{2,1,0:T(8,128)(2,1)S(1)}, bf16[1536,128]{1,0:T(8,128)(2,1)S(1)}, bf16[1536,128]{1,0:T(8,128)(2,1)S(1)}, /*index=5*/s32[]{:T(128)}) while((s32[]{:T(128)}, bf16[3,512,128]{2,1,0:T(8,128)(2,1)S(1)}, bf16[3,512,128]{2,1,0:T(8,128)(2,1)S(1)}, ...), condition=%wide.region_6.6_spmd, body=%wide.region_3.5_spmd.sunk | while | flops 408222720 | bytes 10496077 | solution.py:76
  383.6 1.6 dynamic-slice_bitcast_fusion.2
  385.5 6.1 %while.33 = (s32[]{:T(128)}, bf16[3,512,128]{2,1,0:T(8,128)(2,1)S(1)}, bf16[3,512,128]{2,1,0:T(8,128)(2,1)S(1)}, bf16[1536,128]{1,0:T(8,128)(2,1)S(1)}, bf16[1536,128]{1,0:T(8,128)(2,1)S(1)}, /*index=5*/s32[]{:T(128)}) while((s32[]{:T(128)}, bf16[3,512,128]{2,1,0:T(8,128)(2,1)S(1)}, bf16[3,512,128]{2,1,0:T(8,128)(2,1)S(1)}, ...), condition=%wide.region_6.6_spmd, body=%wide.region_3.5_spmd.sunk | while | flops 408222720 | bytes 10496077 | solution.py:76
  392.4 1.5 dynamic-slice_bitcast_fusion.2
  394.1 6.1 %while.33 = (s32[]{:T(128)}, bf16[3,512,128]{2,1,0:T(8,128)(2,1)S(1)}, bf16[3,512,128]{2,1,0:T(8,128)(2,1)S(1)}, bf16[1536,128]{1,0:T(8,128)(2,1)S(1)}, bf16[1536,128]{1,0:T(8,128)(2,1)S(1)}, /*index=5*/s32[]{:T(128)}) while((s32[]{:T(128)}, bf16[3,512,128]{2,1,0:T(8,128)(2,1)S(1)}, bf16[3,512,128]{2,1,0:T(8,128)(2,1)S(1)}, ...), condition=%wide.region_6.6_spmd, body=%wide.region_3.5_spmd.sunk | while | flops 408222720 | bytes 10496077 | solution.py:76
  401.0 8.2 %copy.103 = bf16[3,1536,128]{2,0,1:T(4,128)(2,1)} copy(bf16[3,1536,128]{2,1,0:T(8,128)(2,1)} %get-tuple-element.69) | data formatting | bytes 2359296 | tf_op jit(solution)/shard_map/while | solution.py:81
  409.2 7.1 %all-to-all-start.2 = ((bf16[1,3,1536,128]{3,1,0,2:T(4,128)(2,1)}), bf16[1,3,1536,128]{3,1,0,2:T(4,128)(2,1)}, u32[]{:S(2)}, u32[]{:S(2)}) async-start(bf16[1,3,1536,128]{3,1,0,2:T(4,128)(2,1)} %bitcast.87), calls=%async_computation.2 | async-start | bytes 3145728 | tf_op jit(solution)/shard_map/all_to_all | solution.py:134
  416.5 22.2 %all-to-all-done.2 = bf16[1,3,1536,128]{3,1,0,2:T(4,128)(2,1)} async-done(((bf16[1,3,1536,128]{3,1,0,2:T(4,128)(2,1)}), bf16[1,3,1536,128]{3,1,0,2:T(4,128)(2,1)}, u32[]{:S(2)}, u32[]{:S(2)}) %all-to-all-start.2) | async-done | bytes 1179680 | tf_op jit(solution)/shard_map/all_to_all | solution.py:134
  438.7 1.6 copy.53
  440.3 1.1 copy.54
  441.4 5.5 %fusion.54 = (f32[8,48]{1,0:T(8,128)S(1)}, f32[8,48,1536]{2,1,0:T(8,128)S(1)}) fusion(f32[8,48,1536]{2,1,0:T(8,128)} %copy-done.3, bf16[1536,1536]{1,0:T(8,128)(2,1)} %all-gather.2.cloned.1.call-done, bf16[8,12,6,8,128]{4,3,2,1,0:T(8,128)(2,1)} %bitcast.89, f32[8,1536]{1,0:T(8,128)S(1)} %copy-done.14), kind=kOutput, calls=%fused_computation.109 | convolution fusion | flops 1813708416 | bytes 10667520 | tf_op jit(solution)/shard_map/tsd,de->tse/dot_general | solution.py:139
  448.0 22.7 %all_gather.7 = f32[8,48,64]{2,1,0:T(8,128)S(1)} all-gather(f32[1,48,64]{2,1,0:T(8,128)S(1)} %slice.39), channel_id=1, replica_groups=mesh['tm'=8,'seq'=32] {'tm'}, dimensions={0}, use_global_device_ids=true | all-gather | bytes 110592 | tf_op jit(solution)/shard_map/all_gather | solution.py:21
  471.5 70.3 %psum.7 = f32[8]{0:T(128)S(1)} all-reduce(f32[8]{0:T(128)S(1)} %get-tuple-element.95), channel_id=1, replica_groups=mesh['tm'=8,'seq'=32] {'seq'}, use_global_device_ids=true, to_apply=%region_14.15 | all-reduce | flops 8 | bytes 64 | tf_op jit(solution)/shard_map/psum | solution.py:157
  (109 shorter events, 33.4 us)
Async XLA Ops:
  7.2 61.0 %copy-start = (bf16[256,4608]{1,0:T(8,128)(2,1)S(1)}, bf16[256,4608]{1,0:T(8,128)(2,1)}, u32[]{:S(2)}) copy-start(bf16[256,4608]{1,0:T(8,128)(2,1)} %param.20) | copy-start | bytes 7077892
  7.2 35.2 %copy-start.2 = (bf16[48,12,384]{2,0,1:T(8,128)(2,1)S(1)}, bf16[48,12,384]{2,0,1:T(8,128)(2,1)}, u32[]{:S(2)}) copy-start(bf16[48,12,384]{2,0,1:T(8,128)(2,1)} %param.21) | copy-start | bytes 1327108
  55.5 8.8 %copy-start.6 = (f32[8,48,64]{2,1,0:T(8,128)S(1)}, f32[8,48,64]{2,1,0:T(8,128)}, u32[]{:S(2)}) copy-start(f32[8,48,64]{2,1,0:T(8,128)} %param.15) | copy-start | bytes 294916
  55.5 12.5 %copy-start.15 = (s32[8]{0:T(128)S(1)}, s32[8]{0:T(128)}, u32[]{:S(2)}) copy-start(s32[8]{0:T(128)} %param.17) | copy-start | bytes 100
  55.5 13.8 %copy-start.12 = (f32[48,64]{1,0:T(8,128)S(1)}, f32[48,64]{1,0:T(8,128)}, u32[]{:S(2)}) copy-start(f32[48,64]{1,0:T(8,128)} %param.16) | copy-start | bytes 36868
  55.5 14.4 %copy-start.11 = (bf16[64,1536]{1,0:T(8,128)(2,1)S(1)}, bf16[64,1536]{1,0:T(8,128)(2,1)}, u32[]{:S(2)}) copy-start(bf16[64,1536]{1,0:T(8,128)(2,1)} %param.19) | copy-start | bytes 589828
  55.5 236.1 %all-to-all-start = ((bf16[1536,12,384]{2,1,0:T(8,128)(2,1)}), bf16[1536,12,384]{2,1,0:T(8,128)(2,1)}, u32[]{:S(2)}, u32[]{:S(2)}) async-start(bf16[1536,12,384]{2,1,0:T(8,128)(2,1)} %copy_dynamic-update-slice_fusion.31), calls=%async_computation | async-start | bytes 37748736 | tf_op jit(solution)/shard_map/all_to_all | solution.py:10
  64.3 5.0 collective-permute-start
  69.3 236.9 %copy-start.4 = (f32[7,48,64]{2,1,0:T(8,128)}, f32[7,48,64]{2,1,0:T(8,128)S(1)}, u32[]{:S(2)}) copy-start(f32[7,48,64]{2,1,0:T(8,128)S(1)} %slice.28) | copy-start | bytes 258052
  69.3 0.6 copy-start.8
  70.4 239.9 %copy-start.3 = (f32[8,48,1536]{2,1,0:T(8,128)}, f32[8,48,1536]{2,1,0:T(8,128)S(1)}, u32[]{:S(2)}) copy-start(f32[8,48,1536]{2,1,0:T(8,128)S(1)} %get-tuple-element.110) | copy-start | bytes 7077892
  310.3 62.6 %all-to-all-start.1 = ((bf16[32,3,48,384]{3,2,1,0:T(8,128)(2,1)}), bf16[32,3,48,384]{3,2,1,0:T(8,128)(2,1)S(1)}, u32[]{:S(2)}, u32[]{:S(2)}) async-start(bf16[32,3,48,384]{3,2,1,0:T(8,128)(2,1)} %bitcast.85), calls=%async_computation.1 | async-start | bytes 7077888 | tf_op jit(solution)/shard_map/all_to_all | solution.py:133
  327.7 113.7 %all-gather.2.cloned.1.call-start = ((), (), s32[]{:S(2)}) async-start(), calls=%async_computation.3 | async-start | bytes 4866048 | tf_op jit(solution)/shard_map/all_gather | solution.py:142
  375.1 41.2 %copy-start.16 = (s32[8]{0:T(128)S(1)}, s32[8]{0:T(128)}, u32[]{:S(2)}) copy-start(s32[8]{0:T(128)} %param.17) | copy-start | bytes 100
  375.1 41.2 %copy-start.17 = (s32[8]{0:T(128)S(1)}, s32[8]{0:T(128)}, u32[]{:S(2)}) copy-start(s32[8]{0:T(128)} %param.18) | copy-start | bytes 100
  375.1 66.3 %copy-start.14 = (f32[8,1536]{1,0:T(8,128)S(1)}, f32[8,1536]{1,0:T(8,128)}, u32[]{:S(2)}) copy-start(f32[8,1536]{1,0:T(8,128)} %get-tuple-element.104) | copy-start | bytes 147460
  401.0 46.4 %copy-start.10 = (bf16[1536,64]{0,1:T(8,128)(2,1)S(1)}, bf16[1536,64]{0,1:T(8,128)(2,1)}, u32[]{:S(2)}) copy-start(bf16[1536,64]{0,1:T(8,128)(2,1)} %param.23) | copy-start | bytes 589828
  401.0 46.9 %copy-start.5 = (f32[7,48,64]{2,1,0:T(8,128)S(1)}, f32[7,48,64]{2,1,0:T(8,128)}, u32[]{:S(2)}) copy-start(f32[7,48,64]{2,1,0:T(8,128)} %copy-done.4) | copy-start | bytes 258052
  401.0 46.9 %copy-start.9 = (f32[1,48,64]{2,1,0:T(8,128)S(1)}, f32[1,48,64]{2,1,0:T(8,128)}, u32[]{:S(2)}) copy-start(f32[1,48,64]{2,1,0:T(8,128)} %copy-done.8) | copy-start | bytes 36868
  401.0 69.7 %copy-start.13 = (f32[48,64]{1,0:T(8,128)S(1)}, f32[48,64]{1,0:T(8,128)}, u32[]{:S(2)}) copy-start(f32[48,64]{1,0:T(8,128)} %param.16) | copy-start | bytes 36868
  401.0 69.8 %copy-start.7 = (f32[8,48,64]{2,1,0:T(8,128)S(1)}, f32[8,48,64]{2,1,0:T(8,128)}, u32[]{:S(2)}) copy-start(f32[8,48,64]{2,1,0:T(8,128)} %param.15) | copy-start | bytes 294916
  401.0 141.3 %copy-start.1 = (bf16[256,4608]{1,0:T(8,128)(2,1)S(1)}, bf16[256,4608]{1,0:T(8,128)(2,1)}, u32[]{:S(2)}) copy-start(bf16[256,4608]{1,0:T(8,128)(2,1)} %param.20) | copy-start | bytes 7077892
  409.2 29.5 %all-to-all-start.2 = ((bf16[1,3,1536,128]{3,1,0,2:T(4,128)(2,1)}), bf16[1,3,1536,128]{3,1,0,2:T(4,128)(2,1)}, u32[]{:S(2)}, u32[]{:S(2)}) async-start(bf16[1,3,1536,128]{3,1,0,2:T(4,128)(2,1)} %bitcast.87), calls=%async_computation.2 | async-start | bytes 3145728 | tf_op jit(solution)/shard_map/all_to_all | solution.py:134
Sparse Core Ops, SparseCore 0:
  331.0 70.2 all-gather.1
